TPU v7x, 128 devices: a whole 4x4x4 slice. The times are simulated.
128 devices in a mesh: seq: 32 (over z, x, core), batch: 4 (over y).
Axes of the slice: x: 4, y: 4, z: 4, core: 2. Of those that a mesh axis runs over, the one named last changes fastest.
Arguments:
- sequence_input: bfloat16 [32768, 1536], P(('batch', 'seq')), parts along dimension 0, may hold values from -6 to 6
- conv_first: bfloat16 [5, 1536, 768], replicated, may hold values from -0.0625 to 0.0625
- conv_second: bfloat16 [5, 768, 768], replicated, may hold values from -0.09375 to 0.09375
- qkv_weight: bfloat16 [768, 1536], replicated, may hold values from -0.21875 to 0.21875
- out_weight: bfloat16 [512, 768], replicated, may hold values from -0.25 to 0.25
- logit_scale: float32 [4], replicated, may hold values from 2.5 to 30, as said below
Outputs:
- block_output: bfloat16 [32768, 768], P(('batch', 'seq')), parts along dimension 0
There are 4 independent parts, one for each index of `batch`. A program takes and returns all parts, laid end to end along the dimension named above; an argument that names none is the same for every part. Nothing has to cross between parts.
Inputs may be any that keep to these rules, and one draw needn't show every extreme that they name: `logit_scale`: one positive scale a head.
All inputs are finite; a program needn't handle non-finite values.
Results may differ from a plain program's by a relative error of at most 0.023.
Values may be sent and summed in bfloat16 or wider, within the bound.
A program may use at most 256 MiB of HBM per device.

v0:
```python
import math
import jax
import jax.numpy as jnp
from jax import lax
from jax.sharding import PartitionSpec as P


def padded_2(block, sides, width):
    for axis, dim in sides:
        count = lax.axis_size(axis)
        forward = [(i, i + 1) for i in range(count - 1)]
        backward = [(target, source) for source, target in forward]
        low = lax.ppermute(
            lax.slice_in_dim(block, block.shape[dim] - width, None, axis=dim), axis, forward
        )
        high = lax.ppermute(lax.slice_in_dim(block, 0, width, axis=dim), axis, backward)
        block = jnp.concatenate([low, block, high], axis=dim)
    return block


def convolve(padded, weight, row_count):
    conv_sum = jnp.dot(padded[0:row_count], weight[0], preferred_element_type=jnp.float32)
    for offset in range(1, weight.shape[0]):
        conv_sum = conv_sum + jnp.dot(
            padded[offset : offset + row_count], weight[offset], preferred_element_type=jnp.float32
        )
    return conv_sum


def head_rms(tensor):
    return tensor * lax.rsqrt(jnp.mean(tensor * tensor, axis=-1, keepdims=True) + 1e-06)


def attend_block(state_now, queries, key_block, value_block):
    running_max, running_sum, running_out = state_now
    scores = jnp.einsum("thd,shd->hts", queries, key_block, preferred_element_type=jnp.float32)
    new_max = jnp.maximum(running_max, jnp.max(scores, axis=2))
    weights = jnp.exp(scores - new_max[:, :, None])
    running_sum = jnp.sum(weights, axis=2)
    running_out = jnp.einsum(
        "hts,shd->htd",
        weights.astype(jnp.bfloat16),
        value_block,
        preferred_element_type=jnp.float32,
    )
    return (new_max, running_sum, running_out)


def body(sequence_input, conv_first, conv_second, qkv_weight, out_weight, logit_scale):
    row_count = sequence_input.shape[0]
    padded_input = padded_2(sequence_input, (("seq", 0),), 2)
    first_out = jax.nn.gelu(convolve(padded_input, conv_first, row_count)).astype(jnp.bfloat16)
    padded_first = padded_2(first_out, (("seq", 0),), 2)
    second = convolve(padded_first, conv_second, row_count)
    hidden = (first_out.astype(jnp.float32) + second).astype(jnp.bfloat16)
    head_count = logit_scale.shape[0]
    width_all = qkv_weight.shape[1] // 3
    head_size = width_all // head_count
    query_part = jnp.dot(hidden, qkv_weight[:, :width_all], preferred_element_type=jnp.float32)
    query_part = query_part.reshape(row_count, head_count, head_size)
    queries = (head_rms(query_part) * (logit_scale / math.sqrt(head_size))[None, :, None]).astype(
        jnp.bfloat16
    )
    kv_weight = qkv_weight[:, width_all:]
    start_state = (
        jnp.full((head_count, row_count), -1e30, jnp.float32),
        jnp.zeros((head_count, row_count), jnp.float32),
        jnp.zeros((head_count, row_count, head_size), jnp.float32),
    )
    piece_rows = hidden.shape[0]
    paired = jnp.dot(hidden, kv_weight, preferred_element_type=jnp.float32)
    key_block = head_rms(paired[:, :width_all].reshape(piece_rows, head_count, head_size)).astype(
        jnp.bfloat16
    )
    value_block = (
        paired[:, width_all:].reshape(piece_rows, head_count, head_size).astype(jnp.bfloat16)
    )
    own_keys = key_block
    own_values = value_block
    flat_keys = own_keys.reshape(row_count, width_all)
    flat_values = own_values.reshape(row_count, width_all)
    piece_pair = (
        lax.all_gather(flat_keys, "seq", axis=0, tiled=True),
        lax.all_gather(flat_values, "seq", axis=0, tiled=True),
    )
    piece_rows = piece_pair[0].shape[0]
    key_block = piece_pair[0].reshape(piece_rows, head_count, head_size)
    value_block = piece_pair[1].reshape(piece_rows, head_count, head_size)
    final_state = attend_block(start_state, queries, key_block, value_block)
    running_max, running_sum, running_out = final_state
    attended = (
        (running_out / running_sum[:, :, None])
        .transpose(1, 0, 2)
        .reshape(row_count, width_all)
        .astype(jnp.bfloat16)
    )
    return (
        hidden.astype(jnp.float32)
        + jnp.dot(attended, out_weight, preferred_element_type=jnp.float32)
    ).astype(jnp.bfloat16)


def solution(mesh):
    in_specs = (P(("batch", "seq"), None), P(), P(), P(), P(), P())
    out_specs = P(("batch", "seq"), None)
    return jax.shard_map(body, mesh=mesh, in_specs=in_specs, out_specs=out_specs, check_vma=False)
```

profile of v0, /device:TPU:1, one launch (start us, length us, event | category | flops | bytes accessed | tf_op | source)
XLA Modules:
  0.0 185.4 jit_solution(1731052009252895028)
XLA Ops:
  6.5 0.8 fusion.101
  7.4 3.3 %collective-permute-start.1 = (bf16[2,1536]{1,0:T(2,128)(2,1)S(1)}, bf16[2,1536]{1,0:T(2,128)(2,1)S(1)}, u32[]{:S(2)}, u32[]{:S(2)}) collective-permute-start(bf16[2,1536]{1,0:T(2,128)(2,1)S(1)} %get-tuple-element.6), channel_id=1, source_target_pairs={{4,0},{8,4},{12,8},{16,12},{20,16},{24,20},{28,24},{32,28},{36,32}... | collective-permute-start | bytes 18440 | tf_op jit(solution)/shard_map/ppermute | solution.py:16
  10.7 3.5 %collective-permute-start = (bf16[2,1536]{1,0:T(2,128)(2,1)S(1)}, bf16[2,1536]{1,0:T(2,128)(2,1)S(1)}, u32[]{:S(2)}, u32[]{:S(2)}) collective-permute-start(bf16[2,1536]{1,0:T(2,128)(2,1)S(1)} %get-tuple-element.5), channel_id=1, source_target_pairs={{0,4},{4,8},{8,12},{12,16},{16,20},{20,24},{24,28},{28,32},{32,36}... | collective-permute-start | bytes 18440 | tf_op jit(solution)/shard_map/ppermute | solution.py:13
  14.2 2.7 %fusion.12 = f32[256,768]{1,0:T(8,128)S(1)} fusion(bf16[256,1536]{1,0:T(8,128)(2,1)} %param.6, bf16[5,1536,768]{2,1,0:T(8,128)(2,1)} %param.7), kind=kOutput, calls=%fused_computation.12 | convolution fusion | flops 603979776 | bytes 3932160 | tf_op jit(solution)/shard_map/dot_general | solution.py:24
  16.9 1.2 constant_dynamic-update-slice_fusion.1
  18.2 2.5 %fusion.8 = f32[256,768]{1,0:T(8,128)S(1)} fusion(bf16[5,1536,768]{2,1,0:T(8,128)(2,1)} %param.7, bf16[258,1536]{1,0:T(8,128)(2,1)S(1)} %constant_dynamic-update-slice_fusion), kind=kOutput, calls=%fused_computation.8 | convolution fusion | flops 603979776 | bytes 3932160 | tf_op jit(solution)/shard_map/dot_general | solution.py:24
  20.7 0.8 fusion.10
  21.5 0.8 fusion.14
  22.4 1.0 fusion.77
  23.4 2.9 %collective-permute-start.2 = (bf16[2,768]{1,0:T(2,128)(2,1)S(1)}, bf16[2,768]{1,0:T(2,128)(2,1)S(1)}, u32[]{:S(2)}, u32[]{:S(2)}) collective-permute-start(bf16[2,768]{1,0:T(2,128)(2,1)S(1)} %get-tuple-element.7), channel_id=1, source_target_pairs={{0,4},{4,8},{8,12},{12,16},{16,20},{20,24},{24,28},{28,32},{32,36}... | collective-permute-start | bytes 9224 | tf_op jit(solution)/shard_map/ppermute | solution.py:13
  26.8 1.9 %collective-permute-start.3 = (bf16[2,768]{1,0:T(2,128)(2,1)S(1)}, bf16[2,768]{1,0:T(2,128)(2,1)S(1)}, u32[]{:S(2)}, u32[]{:S(2)}) collective-permute-start(bf16[2,768]{1,0:T(2,128)(2,1)S(1)} %get-tuple-element.8), channel_id=1, source_target_pairs={{4,0},{8,4},{12,8},{16,12},{20,16},{24,20},{28,24},{32,28},{36,32}... | collective-permute-start | bytes 9224 | tf_op jit(solution)/shard_map/ppermute | solution.py:16
  29.3 2.5 %collective-permute-done.3 = bf16[2,768]{1,0:T(2,128)(2,1)S(1)} collective-permute-done((bf16[2,768]{1,0:T(2,128)(2,1)S(1)}, bf16[2,768]{1,0:T(2,128)(2,1)S(1)}, u32[]{:S(2)}, u32[]{:S(2)}) %collective-permute-start.3) | collective-permute-done | bytes 3104 | tf_op jit(solution)/shard_map/ppermute | solution.py:16
  32.8 0.5 fusion.40
  33.3 0.6 fusion.23
  34.9 0.8 fusion.87
  35.9 0.7 slice.220
  36.7 1.5 fusion.85
  39.1 55.5 %all-gather.3.cloned.1.call-done = bf16[8192,512]{1,0:T(8,128)(2,1)} async-done(((bf16[256,512]{1,0:T(8,128)(2,1)}), bf16[8192,512]{1,0:T(8,128)(2,1)}) %all-gather.3.cloned.1.call-update) | async-done | bytes 8388624 | tf_op jit(solution)/shard_map/all_gather | solution.py:83
  94.6 16.8 %fusion.103 = (f32[4,256]{1,0:T(4,128)S(1)}, f32[4,256,8192]{2,1,0:T(8,128)}) fusion(bf16[256,4,128]{2,1,0:T(4,128)(2,1)S(1)} %multiply_convert_fusion, bf16[8192,512]{1,0:T(8,128)(2,1)} %all-gather.3.cloned.1.call-done), kind=kOutput, calls=%fused_computation.102 | convolution fusion | flops 2155871232 | bytes 42209280 | tf_op jit(solution)/shard_map/thd,shd->hts/dot_general | solution.py:36
  111.4 13.7 %fusion = f32[4,256]{1,0:T(4,128)S(1)} fusion(f32[4,256,8192]{2,1,0:T(8,128)} %get-tuple-element.10, f32[4,256]{1,0:T(4,128)S(1)} %broadcast_maximum_fusion), kind=kLoop, calls=%fused_computation.1 | loop fusion | flops 16776192 | bytes 33562624 | tf_op jit(solution)/shard_map/reduce_sum | solution.py:39
  125.2 24.3 %all-gather.5.cloned.1.call-done = bf16[8192,512]{1,0:T(8,128)(2,1)} async-done(((bf16[256,512]{1,0:T(8,128)(2,1)}), bf16[8192,512]{1,0:T(8,128)(2,1)}) %all-gather.5.cloned.1.call-update) | async-done | bytes 8388624 | tf_op jit(solution)/shard_map/all_gather | solution.py:84
  149.4 12.0 %copy.21 = bf16[8192,512]{0,1:T(8,128)(2,1)} copy(bf16[8192,512]{1,0:T(8,128)(2,1)} %all-gather.5.cloned.1.call-done) | data formatting | bytes 16777216 | tf_op jit(solution)/shard_map/reshape | solution.py:88
  161.4 16.0 %fusion.48 = bf16[256,4,128]{0,2,1:T(8,128)(2,1)S(1)} fusion(bf16[8192,4,128]{0,2,1:T(8,128)(2,1)} %bitcast.72, f32[4,256,8192]{2,1,0:T(8,128)} %get-tuple-element.10, f32[4,256]{1,0:T(4,128)S(1)} %broadcast_maximum_fusion, f32[256,4]{0,1:T(4,128)S(1)} %bitcast.77), kind=kOutput, calls=%fused_computation.39 | convolution fusion | flops 2164523008 | bytes 42213376 | tf_op jit(solution)/shard_map/hts,shd->htd/dot_general | solution.py:40
  177.5 1.1 fusion.41
  (39 shorter events, 4.1 us)
Async XLA Ops:
  6.5 170.9 %copy-start = (bf16[512,768]{1,0:T(8,128)(2,1)S(1)}, bf16[512,768]{1,0:T(8,128)(2,1)}, u32[]{:S(2)}) copy-start(bf16[512,768]{1,0:T(8,128)(2,1)} %param.10) | copy-start | bytes 2359300
  6.5 88.1 %all-gather.3.cloned.1.call-start = ((), (), s32[]{:S(2)}) async-start(), calls=%async_computation | async-start | bytes 8650752 | tf_op jit(solution)/shard_map/all_gather | solution.py:83
  7.4 10.8 %collective-permute-start.1 = (bf16[2,1536]{1,0:T(2,128)(2,1)S(1)}, bf16[2,1536]{1,0:T(2,128)(2,1)S(1)}, u32[]{:S(2)}, u32[]{:S(2)}) collective-permute-start(bf16[2,1536]{1,0:T(2,128)(2,1)S(1)} %get-tuple-element.6), channel_id=1, source_target_pairs={{4,0},{8,4},{12,8},{16,12},{20,16},{24,20},{28,24},{32,28},{36,32}... | collective-permute-start | bytes 18440 | tf_op jit(solution)/shard_map/ppermute | solution.py:16
  10.7 10.0 %copy-start.3 = (bf16[5,1536,768]{2,1,0:T(8,128)(2,1)S(1)}, bf16[5,1536,768]{2,1,0:T(8,128)(2,1)}, u32[]{:S(2)}) copy-start(bf16[5,1536,768]{2,1,0:T(8,128)(2,1)} %param.7) | copy-start | bytes 35389444
  10.7 10.8 %collective-permute-start = (bf16[2,1536]{1,0:T(2,128)(2,1)S(1)}, bf16[2,1536]{1,0:T(2,128)(2,1)S(1)}, u32[]{:S(2)}, u32[]{:S(2)}) collective-permute-start(bf16[2,1536]{1,0:T(2,128)(2,1)S(1)} %get-tuple-element.5), channel_id=1, source_target_pairs={{0,4},{4,8},{8,12},{12,16},{16,20},{20,24},{24,28},{28,32},{32,36}... | collective-permute-start | bytes 18440 | tf_op jit(solution)/shard_map/ppermute | solution.py:13
  18.1 3.4 %copy-start.2 = (bf16[256,1536]{1,0:T(8,128)(2,1)S(1)}, bf16[256,1536]{1,0:T(8,128)(2,1)}, u32[]{:S(2)}) copy-start(bf16[256,1536]{1,0:T(8,128)(2,1)} %param.6) | copy-start | bytes 2359300
  21.5 4.8 %slice-start = ((s8[5898240]{0:T(1024)(128)(4,1)}), s8[4194304]{0:T(1024)(128)(4,1)S(1)}, s32[]{:S(2)}) async-start(s8[5898240]{0:T(1024)(128)(4,1)} %bitcast.73), calls=%async_computation.2 | async-start | bytes 8388608
  22.4 4.0 %slice-start.1 = ((s8[5898240]{0:T(1024)(128)(4,1)}), s8[1703936]{0:T(1024)(128)(4,1)S(1)}, s32[]{:S(2)}) async-start(s8[5898240]{0:T(1024)(128)(4,1)} %bitcast.73), calls=%async_computation.3 | async-start | bytes 3407872
  23.4 5.4 %collective-permute-start.2 = (bf16[2,768]{1,0:T(2,128)(2,1)S(1)}, bf16[2,768]{1,0:T(2,128)(2,1)S(1)}, u32[]{:S(2)}, u32[]{:S(2)}) collective-permute-start(bf16[2,768]{1,0:T(2,128)(2,1)S(1)} %get-tuple-element.7), channel_id=1, source_target_pairs={{0,4},{4,8},{8,12},{12,16},{16,20},{20,24},{24,28},{28,32},{32,36}... | collective-permute-start | bytes 9224 | tf_op jit(solution)/shard_map/ppermute | solution.py:13
  26.8 4.9 %collective-permute-start.3 = (bf16[2,768]{1,0:T(2,128)(2,1)S(1)}, bf16[2,768]{1,0:T(2,128)(2,1)S(1)}, u32[]{:S(2)}, u32[]{:S(2)}) collective-permute-start(bf16[2,768]{1,0:T(2,128)(2,1)S(1)} %get-tuple-element.8), channel_id=1, source_target_pairs={{4,0},{8,4},{12,8},{16,12},{20,16},{24,20},{28,24},{32,28},{36,32}... | collective-permute-start | bytes 9224 | tf_op jit(solution)/shard_map/ppermute | solution.py:16
  29.3 4.0 %copy-start.1 = (bf16[768,1536]{1,0:T(8,128)(2,1)S(1)}, bf16[768,1536]{1,0:T(8,128)(2,1)}, u32[]{:S(2)}) copy-start(bf16[768,1536]{1,0:T(8,128)(2,1)} %param.9) | copy-start | bytes 7077892
  32.8 3.9 %copy-start.4 = (f32[4]{0:T(128)S(1)}, f32[4]{0:T(128)}, u32[]{:S(2)}) copy-start(f32[4]{0:T(128)} %param.11) | copy-start | bytes 52
  35.7 113.8 %all-gather.5.cloned.1.call-start = ((), (), s32[]{:S(2)}) async-start(), calls=%async_computation.1 | async-start | bytes 8650752 | tf_op jit(solution)/shard_map/all_gather | solution.py:84
Sparse Core Ops, SparseCore 0:
  35.8 58.7 all-gather.2
  96.9 52.5 all-gather.4
where the time goes:
time: 186 us; the launch traced here: 185 us
  waiting for transfers between devices  82.3 us (44%)
  matrix products  46.4 us (25%)
  other arithmetic  15.6 us (8%)
  local copies, waits for them, and re-layouts  15.5 us (8%)
  between operations  13.8 us (7%)
  starting transfers between devices  11.9 us (6%)
    all_gather x1, waiting for transfers between devices, body(): lax.all_gather(flat_keys, 'seq', axis=0, tiled=True)  55.5 us
    all_gather x1, waiting for transfers between devices, body(): lax.all_gather(flat_values, 'seq', axis=0, tiled=True)  24.3 us
    dot_general x1, matrix products, attend_block(): jnp.einsum('thd,shd->hts', queries, key_block, preferred_element_type=jnp...  16.8 us
    dot_general x1, matrix products, attend_block(): jnp.einsum('hts,shd->htd', weights.astype(jnp.bfloat16), value_block, pre...  16 us
    reduce_sum x1, other arithmetic, attend_block(): running_sum = jnp.sum(weights, axis=2)  13.7 us
    reshape x1, local copies, waits for them, and re-layouts, body(): value_block = piece_pair[1].reshape(piece_rows, head_count, head_size)  12 us
    dot_general x8, matrix products, convolve(): jnp.dot(padded[offset:offset + row_count], weight[offset], preferred_elem...  8.8 us
    ppermute x2, starting transfers between devices, padded_2(): lax.ppermute(lax.slice_in_dim(block, block.shape[dim] - width, None, axis...  6.42 us
  transfers between devices with their start and end apart: 6, of which 3 were waited for; matrix products, arithmetic and copies ran while one was open for 23% of the time, Pallas kernels for 0%

commit v1 on v0

--- a/solution.py
+++ b/solution.py
@@ -79,10 +79,10 @@
     own_values = value_block
     flat_keys = own_keys.reshape(row_count, width_all)
     flat_values = own_values.reshape(row_count, width_all)
-    piece_pair = (
-        lax.all_gather(flat_keys, "seq", axis=0, tiled=True),
-        lax.all_gather(flat_values, "seq", axis=0, tiled=True),
+    lay_the_sites = lambda a0: jnp.concatenate(
+        jax.lax.all_to_all(jnp.stack(jax.lax.psum(1, "seq") * [a0]), "seq", 0, 0), axis=0
     )
+    piece_pair = (lay_the_sites(flat_keys), lax.all_gather(flat_values, "seq", axis=0, tiled=True))
     piece_rows = piece_pair[0].shape[0]
     key_block = piece_pair[0].reshape(piece_rows, head_count, head_size)
     value_block = piece_pair[1].reshape(piece_rows, head_count, head_size)

time: 186 us -> 263 us (1.41)
  the two profiles are of different devices: /device:TPU:1 before, /device:TPU:0 now
where the time goes in v1:
time: 263 us; the launch traced here: 262 us
  waiting for transfers between devices  120 us (46%)
  matrix products  46.1 us (18%)
  local copies, waits for them, and re-layouts  44.7 us (17%)
  starting transfers between devices  23.2 us (9%)
  other arithmetic  14.9 us (6%)
  between operations  13.8 us (5%)
    all_to_all x1, waiting for transfers between devices, body(): jax.lax.all_to_all(jnp.stack(jax.lax.psum(1, 'seq') * [a0]), 'seq', 0, 0)  118 us
    dot_general x1, matrix products, attend_block(): jnp.einsum('thd,shd->hts', queries, key_block, preferred_element_type=jnp...  16.5 us
    dot_general x1, matrix products, attend_block(): jnp.einsum('hts,shd->htd', weights.astype(jnp.bfloat16), value_block, pre...  16 us
    all_to_all x1, starting transfers between devices, body(): jax.lax.all_to_all(jnp.stack(jax.lax.psum(1, 'seq') * [a0]), 'seq', 0, 0)  14.1 us
    reduce_sum x1, other arithmetic, attend_block(): running_sum = jnp.sum(weights, axis=2)  13.6 us
    another operation x1, local copies, waits for them, and re-layouts, body(): key_block = piece_pair[0].reshape(piece_rows, head_count, head_size)  13.4 us
    reshape x1, local copies, waits for them, and re-layouts, body(): value_block = piece_pair[1].reshape(piece_rows, head_count, head_size)  12 us
    all_to_all x1, local copies, waits for them, and re-layouts, body(): jax.lax.all_to_all(jnp.stack(jax.lax.psum(1, 'seq') * [a0]), 'seq', 0, 0)  11.4 us
  transfers between devices with their start and end apart: 6, of which 2 were waited for; matrix products, arithmetic and copies ran while one was open for 27% of the time, Pallas kernels for 0%

profile of v1, /device:TPU:0, one launch (start us, length us, event | category | flops | bytes accessed | tf_op | source)
XLA Modules:
  0.0 262.2 jit_solution(4857593313068001192)
XLA Ops:
  6.5 0.8 fusion.99
  7.4 1.3 collective-permute-start.1
  8.7 3.4 %collective-permute-start = (bf16[2,1536]{1,0:T(2,128)(2,1)S(1)}, bf16[2,1536]{1,0:T(2,128)(2,1)S(1)}, u32[]{:S(2)}, u32[]{:S(2)}) collective-permute-start(bf16[2,1536]{1,0:T(2,128)(2,1)S(1)} %get-tuple-element.5), channel_id=1, source_target_pairs={{0,4},{4,8},{8,12},{12,16},{16,20},{20,24},{24,28},{28,32},{32,36}... | collective-permute-start | bytes 18440 | tf_op jit(solution)/shard_map/ppermute | solution.py:13
  12.1 2.7 %fusion.9 = f32[256,768]{1,0:T(8,128)S(1)} fusion(bf16[256,1536]{1,0:T(8,128)(2,1)} %param.6, bf16[5,1536,768]{2,1,0:T(8,128)(2,1)} %param.7), kind=kOutput, calls=%fused_computation.9 | convolution fusion | flops 603979776 | bytes 3932160 | tf_op jit(solution)/shard_map/dot_general | solution.py:24
  14.8 1.2 constant_dynamic-update-slice_fusion.1
  16.1 2.5 fusion.5
  18.6 0.8 fusion.7
  19.4 0.8 fusion.11
  20.3 1.0 fusion.74
  21.3 3.1 %collective-permute-start.2 = (bf16[2,768]{1,0:T(2,128)(2,1)S(1)}, bf16[2,768]{1,0:T(2,128)(2,1)S(1)}, u32[]{:S(2)}, u32[]{:S(2)}) collective-permute-start(bf16[2,768]{1,0:T(2,128)(2,1)S(1)} %get-tuple-element.7), channel_id=1, source_target_pairs={{0,4},{4,8},{8,12},{12,16},{16,20},{20,24},{24,28},{28,32},{32,36}... | collective-permute-start | bytes 9224 | tf_op jit(solution)/shard_map/ppermute | solution.py:13
  24.9 1.3 collective-permute-start.3
  26.7 1.8 collective-permute-done.3
  30.6 0.7 slice.220
  32.6 4.2 %stack.3 = bf16[32,256,512]{1,2,0:T(8,128)(2,1)} broadcast(bf16[256,512]{0,1:T(8,128)(2,1)S(1)} %copy.24), dimensions={1,2} | broadcast | bytes 8650752 | tf_op jit(solution)/shard_map/stack | solution.py:83
  36.7 14.1 %all-to-all-start = ((bf16[32,256,512]{1,2,0:T(8,128)(2,1)}), bf16[32,256,512]{1,2,0:T(8,128)(2,1)}, u32[]{:S(2)}, u32[]{:S(2)}) async-start(bf16[32,256,512]{1,2,0:T(8,128)(2,1)} %stack.3), calls=%async_computation | async-start | bytes 16777216 | tf_op jit(solution)/shard_map/all_to_all | solution.py:83
  50.8 1.5 fusion.82
  53.3 117.9 %all-to-all-done = bf16[32,256,512]{1,2,0:T(8,128)(2,1)} async-done(((bf16[32,256,512]{1,2,0:T(8,128)(2,1)}), bf16[32,256,512]{1,2,0:T(8,128)(2,1)}, u32[]{:S(2)}, u32[]{:S(2)}) %all-to-all-start) | async-done | bytes 8388640 | tf_op jit(solution)/shard_map/all_to_all | solution.py:83
  171.1 11.4 %copy.25 = bf16[32,256,512]{1,0,2:T(8,128)(2,1)} copy(bf16[32,256,512]{1,2,0:T(8,128)(2,1)} %all-to-all-done) | data formatting | bytes 16777216 | tf_op jit(solution)/shard_map/all_to_all | solution.py:83
  182.5 13.4 %reshape_reshape.3 = bf16[8192,4,128]{0,2,1:T(8,128)(2,1)} reshape(bf16[32,256,512]{1,0,2:T(8,128)(2,1)} %copy.25) | data formatting | bytes 16777216 | tf_op jit(solution)/shard_map/reshape;reshape | solution.py:87
  196.0 16.5 %fusion.101 = (f32[4,256]{1,0:T(4,128)S(1)}, f32[4,256,8192]{2,1,0:T(8,128)}) fusion(bf16[8192,4,128]{0,2,1:T(8,128)(2,1)} %reshape_reshape.3, bf16[256,4,128]{2,1,0:T(4,128)(2,1)S(1)} %multiply_convert_fusion), kind=kOutput, calls=%fused_computation.100 | convolution fusion | flops 2155871232 | bytes 42209280 | tf_op jit(solution)/shard_map/thd,shd->hts/dot_general | solution.py:36
  212.5 13.6 %fusion = f32[4,256]{1,0:T(4,128)S(1)} fusion(f32[4,256,8192]{2,1,0:T(8,128)} %get-tuple-element.10, f32[4,256]{1,0:T(4,128)S(1)} %broadcast_maximum_fusion), kind=kLoop, calls=%fused_computation.1 | loop fusion | flops 16776192 | bytes 33562624 | tf_op jit(solution)/shard_map/reduce_sum | solution.py:39
  226.2 12.0 %copy.30 = bf16[8192,512]{0,1:T(8,128)(2,1)} copy(bf16[8192,512]{1,0:T(8,128)(2,1)} %all-gather.2.cloned.1.call-done) | data formatting | bytes 16777216 | tf_op jit(solution)/shard_map/reshape | solution.py:88
  238.2 16.0 %fusion.45 = bf16[256,4,128]{0,2,1:T(8,128)(2,1)S(1)} fusion(bf16[8192,4,128]{0,2,1:T(8,128)(2,1)} %bitcast.66, f32[4,256,8192]{2,1,0:T(8,128)} %get-tuple-element.10, f32[4,256]{1,0:T(4,128)S(1)} %broadcast_maximum_fusion, f32[256,4]{0,1:T(4,128)S(1)} %bitcast.71), kind=kOutput, calls=%fused_computation.36 | convolution fusion | flops 2164523008 | bytes 42213376 | tf_op jit(solution)/shard_map/hts,shd->htd/dot_general | solution.py:40
  254.3 1.1 fusion.38
  (42 shorter events, 5.2 us)
Async XLA Ops:
  6.5 247.7 %copy-start = (bf16[512,768]{1,0:T(8,128)(2,1)S(1)}, bf16[512,768]{1,0:T(8,128)(2,1)}, u32[]{:S(2)}) copy-start(bf16[512,768]{1,0:T(8,128)(2,1)} %param.10) | copy-start | bytes 2359300
  6.5 219.6 %all-gather.2.cloned.1.call-start = ((), (), s32[]{:S(2)}) async-start(), calls=%async_computation.1 | async-start | bytes 8650752 | tf_op jit(solution)/shard_map/all_gather | solution.py:85
  7.4 8.7 %collective-permute-start.1 = (bf16[2,1536]{1,0:T(2,128)(2,1)S(1)}, bf16[2,1536]{1,0:T(2,128)(2,1)S(1)}, u32[]{:S(2)}, u32[]{:S(2)}) collective-permute-start(bf16[2,1536]{1,0:T(2,128)(2,1)S(1)} %get-tuple-element.6), channel_id=1, source_target_pairs={{4,0},{8,4},{12,8},{16,12},{20,16},{24,20},{28,24},{32,28},{36,32}... | collective-permute-start | bytes 18440 | tf_op jit(solution)/shard_map/ppermute | solution.py:16
  8.7 9.9 %copy-start.3 = (bf16[5,1536,768]{2,1,0:T(8,128)(2,1)S(1)}, bf16[5,1536,768]{2,1,0:T(8,128)(2,1)}, u32[]{:S(2)}) copy-start(bf16[5,1536,768]{2,1,0:T(8,128)(2,1)} %param.7) | copy-start | bytes 35389444
  8.7 10.7 %collective-permute-start = (bf16[2,1536]{1,0:T(2,128)(2,1)S(1)}, bf16[2,1536]{1,0:T(2,128)(2,1)S(1)}, u32[]{:S(2)}, u32[]{:S(2)}) collective-permute-start(bf16[2,1536]{1,0:T(2,128)(2,1)S(1)} %get-tuple-element.5), channel_id=1, source_target_pairs={{0,4},{4,8},{8,12},{12,16},{16,20},{20,24},{24,28},{28,32},{32,36}... | collective-permute-start | bytes 18440 | tf_op jit(solution)/shard_map/ppermute | solution.py:13
  16.0 3.4 %copy-start.2 = (bf16[256,1536]{1,0:T(8,128)(2,1)S(1)}, bf16[256,1536]{1,0:T(8,128)(2,1)}, u32[]{:S(2)}) copy-start(bf16[256,1536]{1,0:T(8,128)(2,1)} %param.6) | copy-start | bytes 2359300
  19.4 5.0 %slice-start = ((s8[5898240]{0:T(1024)(128)(4,1)}), s8[4194304]{0:T(1024)(128)(4,1)S(1)}, s32[]{:S(2)}) async-start(s8[5898240]{0:T(1024)(128)(4,1)} %bitcast.67), calls=%async_computation.2 | async-start | bytes 8388608
  20.2 4.2 %slice-start.1 = ((s8[5898240]{0:T(1024)(128)(4,1)}), s8[1703936]{0:T(1024)(128)(4,1)S(1)}, s32[]{:S(2)}) async-start(s8[5898240]{0:T(1024)(128)(4,1)} %bitcast.67), calls=%async_computation.3 | async-start | bytes 3407872
  21.3 4.9 %collective-permute-start.2 = (bf16[2,768]{1,0:T(2,128)(2,1)S(1)}, bf16[2,768]{1,0:T(2,128)(2,1)S(1)}, u32[]{:S(2)}, u32[]{:S(2)}) collective-permute-start(bf16[2,768]{1,0:T(2,128)(2,1)S(1)} %get-tuple-element.7), channel_id=1, source_target_pairs={{0,4},{4,8},{8,12},{12,16},{16,20},{20,24},{24,28},{28,32},{32,36}... | collective-permute-start | bytes 9224 | tf_op jit(solution)/shard_map/ppermute | solution.py:13
  24.9 3.6 %collective-permute-start.3 = (bf16[2,768]{1,0:T(2,128)(2,1)S(1)}, bf16[2,768]{1,0:T(2,128)(2,1)S(1)}, u32[]{:S(2)}, u32[]{:S(2)}) collective-permute-start(bf16[2,768]{1,0:T(2,128)(2,1)S(1)} %get-tuple-element.8), channel_id=1, source_target_pairs={{4,0},{8,4},{12,8},{16,12},{20,16},{24,20},{28,24},{32,28},{36,32}... | collective-permute-start | bytes 9224 | tf_op jit(solution)/shard_map/ppermute | solution.py:16
  26.7 3.3 %copy-start.1 = (bf16[768,1536]{1,0:T(8,128)(2,1)S(1)}, bf16[768,1536]{1,0:T(8,128)(2,1)}, u32[]{:S(2)}) copy-start(bf16[768,1536]{1,0:T(8,128)(2,1)} %param.9) | copy-start | bytes 7077892
  36.7 14.1 %copy-start.4 = (f32[4]{0:T(128)S(1)}, f32[4]{0:T(128)}, u32[]{:S(2)}) copy-start(f32[4]{0:T(128)} %param.11) | copy-start | bytes 52
  36.7 134.4 %all-to-all-start = ((bf16[32,256,512]{1,2,0:T(8,128)(2,1)}), bf16[32,256,512]{1,2,0:T(8,128)(2,1)}, u32[]{:S(2)}, u32[]{:S(2)}) async-start(bf16[32,256,512]{1,2,0:T(8,128)(2,1)} %stack.3), calls=%async_computation | async-start | bytes 16777216 | tf_op jit(solution)/shard_map/all_to_all | solution.py:83
Sparse Core Ops, SparseCore 0:
  31.5 135.2 all-gather.1
